TPU v7x, 32 devices: a whole 2x2x4 slice. The times are simulated.
32 devices in a mesh: leaf: 16 (over z, y, x), sub: 2 (over core).
Axes of the slice: x: 2, y: 2, z: 4, core: 2. Of those that a mesh axis runs over, the one named last changes fastest.
Arguments:
- probes: float32 [64, 32768], P(None, ('leaf', 'sub')), may hold values from -600 to 600
- points: float32 [3, 32768], P(None, ('leaf', 'sub')), may hold values from -4 to 4
- leaf_order: int32 [32768], P(('leaf', 'sub')), may hold values from 0 to 1023, as said below
- near_list: int32 [64, 4], P(('leaf', 'sub')), may hold values from 0 to 63, as said below
- far_leaf_list: int32 [64, 2], P(('leaf', 'sub')), may hold values from 0 to 63, as said below
- far_chip_list: int32 [16, 8], P('leaf'), may hold values from -1 to 15, as said below
- leaf_basis: float32 [64, 512, 256], P(('leaf', 'sub')), may hold values from -0.25 to 0.25
- transfer: float32 [64, 256, 256], P(('leaf', 'sub')), may hold values from -0.1875 to 0.1875
- far_leaf_blocks: float32 [128, 256, 256], P(('leaf', 'sub')), may hold values from -0.25 to 0.25
- far_chip_blocks: float32 [128, 256, 256], P('leaf'), may hold values from -0.125 to 0.125
Outputs:
- result: float32 [64, 32768], P(None, ('leaf', 'sub'))
Inputs may be any that keep to these rules, and one draw needn't show every extreme that they name: `leaf_order`: each device's block of 1024 consecutive entries is a permutation of 0 to 1023. `near_list`: row l lists 4 distinct leaves, l among them, all held by the devices l // 2 - 1 to l // 2 + 1 of the joined axis leaf+sub, counted around the cycle. `far_leaf_list`: row l lists the 2 leaves of those same three devices that row l of near_list leaves out. `far_chip_list`: row k lists distinct chip clusters at cycle distance 2 to 5 from k, one to 8 of them, the used entries first and -1 in the rest; some row uses all 8.
All inputs are finite; a program needn't handle non-finite values.
Results may differ from a plain program's by a relative error of at most 0.0003.
Values sent between devices are 32-bit elements; how exact they have to be, the bound alone decides.
No kernel may reach another device: no remote copies, remote signals or barrier semaphores. Data moves between devices by JAX's collectives and lax.ppermute only.
A program may use at most 64 MiB of HBM per device.

v0:
```python
import jax
import jax.numpy as jnp
from jax import lax
from jax.sharding import PartitionSpec as P

CHIP_SPAN = 4
highest = lax.Precision.HIGHEST
inverse_width = 0.5 / (0.15 * 0.15)
epsilon = 1e-06


def from_behind(block, axis, distance):
    devices = range(lax.axis_size(axis))
    route = [((i - distance) % len(devices), i) for i in devices]
    return lax.ppermute(block, axis, route)


def kernel_tiles(source_points, target_points):
    spread = source_points[0] - target_points[0]
    distance = spread * spread
    for coord_axis in (1, 2):
        spread = source_points[coord_axis] - target_points[coord_axis]
        distance = distance + spread * spread
    return jnp.exp(-inverse_width * distance)


def leaf_window(values):
    pieces = []
    for offset in (1, 0, -1):
        if offset == 0:
            pieces.append(values)
        else:
            pieces.append(from_behind(values, ("leaf", "sub"), offset))
    first_device = lax.axis_index(("leaf", "sub")) - 1
    return (jnp.concatenate(pieces, 1), first_device)


def couple_chips(stacked, slot_place, used_count, far_chip_blocks):

    def add_slot(slot_index, running):
        source = stacked[slot_place[slot_index]]
        return running + jnp.dot(
            source,
            far_chip_blocks[slot_index],
            precision=highest,
            preferred_element_type=jnp.float32,
        )

    start_value = jnp.zeros((stacked.shape[1], stacked.shape[2]), jnp.float32)
    return lax.fori_loop(0, used_count, add_slot, start_value)


def chip_level(upward, far_chip_list, far_chip_blocks):
    chip_count = lax.axis_size("leaf")
    chip_index = lax.axis_index("leaf")
    slot_ids = far_chip_list[0]
    used_count = jnp.sum((slot_ids >= 0).astype(jnp.int32))
    offsets = jnp.mod(slot_ids - chip_index, chip_count)
    slot_place = jnp.where(
        offsets <= CHIP_SPAN + 1, offsets - 2, CHIP_SPAN + chip_count - offsets - 2
    )
    slot_place = jnp.clip(slot_place, 0, 2 * CHIP_SPAN - 1)
    shift_list = [-distance for distance in range(2, CHIP_SPAN + 2)] + [
        distance for distance in range(2, CHIP_SPAN + 2)
    ]
    halves = lax.psum_scatter(upward, "sub", scatter_dimension=0, tiled=True)
    pieces = [from_behind(halves, "leaf", offset) for offset in shift_list]
    coupled_half = couple_chips(jnp.stack(pieces), slot_place, used_count, far_chip_blocks)
    coupled = lax.all_gather(coupled_half, "sub", axis=0, tiled=True)
    return coupled


def apply_matrix(
    sorted_values,
    kernels,
    near_index,
    leaf_basis,
    transfer,
    far_leaf_list,
    far_leaf_blocks,
    far_chip_list,
    far_chip_blocks,
    leaf_total,
):
    columns = sorted_values.shape[0]
    leaf_count, leaf_size, rank_size = leaf_basis.shape
    value_window, window_start = leaf_window(sorted_values)
    window_tiles = value_window.reshape(columns, -1, leaf_size)
    source_values = jnp.take(window_tiles, near_index, axis=1)
    near_part = jnp.einsum("clnp,lnpq->clq", source_values, kernels, precision=highest)
    own_tiles = sorted_values.reshape(columns, leaf_count, leaf_size)
    coefficients = jnp.einsum("clp,lpr->lcr", own_tiles, leaf_basis, precision=highest)
    pieces = []
    for offset in (1, 0, -1):
        if offset == 0:
            pieces.append(coefficients)
        else:
            pieces.append(from_behind(coefficients, ("leaf", "sub"), offset))
    coeff_stack = jnp.concatenate(pieces, 0)
    device_index = lax.axis_index(("leaf", "sub"))
    far_index = jnp.mod(far_leaf_list - (device_index - 1) * leaf_count, leaf_total)
    far_sources = jnp.take(coeff_stack, far_index.reshape(-1), axis=0).reshape(
        leaf_count, -1, columns, rank_size
    )
    leaf_blocks = far_leaf_blocks.reshape(leaf_count, -1, rank_size, rank_size)
    local_far = jnp.einsum("ljcr,ljrs->lcs", far_sources, leaf_blocks, precision=highest)
    upward = jnp.einsum("lcr,lrs->cs", coefficients, transfer, precision=highest)
    chip_part = chip_level(upward, far_chip_list, far_chip_blocks)
    downward = local_far + jnp.einsum("cs,lrs->lcr", chip_part, transfer, precision=highest)
    far_part = jnp.einsum("lcr,lpr->clp", downward, leaf_basis, precision=highest)
    return (near_part + far_part).reshape(columns, leaf_count * leaf_size)


def on_device(
    probes,
    points,
    leaf_order,
    near_list,
    far_leaf_list,
    far_chip_list,
    leaf_basis,
    transfer,
    far_leaf_blocks,
    far_chip_blocks,
):
    leaf_count, leaf_size, rank_size = leaf_basis.shape
    leaf_total = leaf_count * lax.axis_size(("leaf", "sub"))
    point_total = probes.shape[1] * lax.axis_size(("leaf", "sub"))
    sorted_probes = probes[:, leaf_order]
    sorted_points = points[:, leaf_order]
    point_window, first_device = leaf_window(sorted_points)
    near_index = jnp.mod(near_list - first_device * leaf_count, leaf_total)
    point_tiles = point_window.reshape(3, -1, leaf_size)
    source_points = jnp.take(point_tiles, near_index, axis=1)
    target_points = sorted_points.reshape(3, leaf_count, leaf_size)
    kernels = kernel_tiles(source_points[..., :, None], target_points[:, :, None, None, :])
    first_pass = apply_matrix(
        sorted_probes,
        kernels,
        near_index,
        leaf_basis,
        transfer,
        far_leaf_list,
        far_leaf_blocks,
        far_chip_list,
        far_chip_blocks,
        leaf_total,
    )
    squares = lax.psum(jnp.sum(first_pass * first_pass, axis=1), ("leaf", "sub"))
    column_scale = lax.rsqrt(squares / point_total + epsilon)
    second = apply_matrix(
        first_pass * column_scale[:, None],
        kernels,
        near_index,
        leaf_basis,
        transfer,
        far_leaf_list,
        far_leaf_blocks,
        far_chip_list,
        far_chip_blocks,
        leaf_total,
    )
    return jnp.zeros_like(second).at[:, leaf_order].set(second)


def solution(mesh):
    return jax.shard_map(
        on_device,
        mesh=mesh,
        in_specs=(
            P(None, ("leaf", "sub")),
            P(None, ("leaf", "sub")),
            P(("leaf", "sub")),
            P(("leaf", "sub"), None),
            P(("leaf", "sub"), None),
            P("leaf", None),
            P(("leaf", "sub"), None, None),
            P(("leaf", "sub"), None, None),
            P(("leaf", "sub"), None, None),
            P("leaf", None, None),
        ),
        out_specs=P(None, ("leaf", "sub")),
        check_vma=False,
    )
```

profile of v0, /device:TPU:5, one launch (start us, length us, event | category | flops | bytes accessed | tf_op | source)
XLA Modules:
  0.0 316.3 jit_solution(15570008534534858504)
XLA Ops:
  9.1 4.0 %gather_fusion.2 = f32[1024,64]{1,0:T(8,128)} fusion(f32[64,1024]{0,1:T(8,128)S(1)} %copy.43, s32[1024]{0:T(1024)S(1)} %get-tuple-element.107), kind=kCustom, calls=%fused_computation.6 | custom fusion | bytes 528384 | tf_op jit(solution)/shard_map/gather | solution.py:129
  13.1 2.1 fusion.58
  17.1 1.8 copy.39
  18.9 3.8 %gather_fusion = f32[1024,3]{1,0:T(8,128)S(1)} fusion(f32[3,1024]{0,1:T(8,128)} %copy.39, s32[1024]{0:T(1024)S(1)} %get-tuple-element.107), kind=kCustom, calls=%fused_computation.4 | custom fusion | bytes 28672 | tf_op jit(solution)/shard_map/gather | solution.py:130
  37.8 1.8 copy.42
  45.1 5.9 %collective-permute-start.6 = (f32[32,256]{1,0:T(8,128)}, f32[32,256]{1,0:T(8,128)S(1)}, u32[]{:S(2)}, u32[]{:S(2)}) collective-permute-start(f32[32,256]{1,0:T(8,128)} %reduce-scatter.3.cloned.1.call-done), channel_id=1, source_target_pairs={{4,0},{6,2},{8,4},{10,6},{12,8},{14,10},{16,12},{18,14},{20,16},{2... | collective-permute-start | bytes 98312 | tf_op jit(solution)/shard_map/ppermute | solution.py:15
  51.8 1.8 collective-permute-start.13
  54.9 10.9 %collective-permute-start.7 = (f32[32,256]{1,0:T(8,128)}, f32[32,256]{1,0:T(8,128)S(1)}, u32[]{:S(2)}, u32[]{:S(2)}) collective-permute-start(f32[32,256]{1,0:T(8,128)} %reduce-scatter.3.cloned.1.call-done), channel_id=1, source_target_pairs={{6,0},{8,2},{10,4},{12,6},{14,8},{16,10},{18,12},{20,14},{22,16},{... | collective-permute-start | bytes 98312 | tf_op jit(solution)/shard_map/ppermute | solution.py:15
  67.3 3.2 %collective-permute-done.8 = f32[32,256]{1,0:T(8,128)S(1)} collective-permute-done((f32[32,256]{1,0:T(8,128)}, f32[32,256]{1,0:T(8,128)S(1)}, u32[]{:S(2)}, u32[]{:S(2)}) %collective-permute-start.8) | collective-permute-done | bytes 32800 | tf_op jit(solution)/shard_map/ppermute | solution.py:15
  70.6 5.1 %collective-permute-start.9 = (f32[32,256]{1,0:T(8,128)}, f32[32,256]{1,0:T(8,128)S(1)}, u32[]{:S(2)}, u32[]{:S(2)}) collective-permute-start(f32[32,256]{1,0:T(8,128)} %reduce-scatter.3.cloned.1.call-done), channel_id=1, source_target_pairs={{10,0},{12,2},{14,4},{16,6},{18,8},{20,10},{22,12},{24,14},{26,16}... | collective-permute-start | bytes 98312 | tf_op jit(solution)/shard_map/ppermute | solution.py:15
  77.0 1.8 collective-permute-start.10
  80.3 2.5 collective-permute-start.11
  82.8 3.7 %collective-permute-done.11 = f32[32,256]{1,0:T(8,128)S(1)} collective-permute-done((f32[32,256]{1,0:T(8,128)}, f32[32,256]{1,0:T(8,128)S(1)}, u32[]{:S(2)}, u32[]{:S(2)}) %collective-permute-start.11) | collective-permute-done | bytes 32800 | tf_op jit(solution)/shard_map/ppermute | solution.py:15
  87.2 38.6 %while.20 = (s32[]{:T(128)}, f32[32,256]{1,0:T(8,128)S(1)}, s32[]{:T(128)}, s32[8]{0:T(128)}, f32[8,32,256]{2,1,0:T(8,128)}, /*index=5*/f32[8,256,256]{2,1,0:T(8,128)}, s32[]{:T(128)}, s32[]{:T(128)}, s32[]{:T(128)}) while((s32[]{:T(128)}, f32[32,256]{1,0:T(8,128)S(1)}, s32[]{:T(128)}, s32[8]{0:T(128)}, f32[8,32,256]{2,1,0:T(8,128)}, ...), condition=%wide.region_3.6_spmd, body=%wide.region_2.5_spmd.sunk | while | flops 25174024 | bytes 360637 | solution.py:50
  125.8 3.8 %all_gather.6 = f32[64,256]{1,0:T(8,128)S(1)} all-gather(f32[32,256]{1,0:T(8,128)S(1)} %get-tuple-element.73), channel_id=1, replica_groups=mesh['leaf'=16,'sub'=2] {'sub'}, dimensions={0}, use_global_device_ids=true | all-gather | bytes 98304 | tf_op jit(solution)/shard_map/all_gather | solution.py:69
  130.3 2.5 pad_maximum_fusion
  132.7 3.6 %gather_fusion.3 = f32[8,64,512]{1,2,0:T(8,128)} fusion(f32[64,6,512]{0,2,1:T(8,128)} %bitcast.168, s32[1024]{0:T(1024)} %pad_clamp_fusion.1), kind=kCustom, calls=%fused_computation.clone | custom fusion | bytes 2097184 | tf_op jit(solution)/shard_map/jit(_take)/gather | solution.py:89
  136.3 3.2 %copy.44 = f32[8,64,512]{2,1,0:T(8,128)} copy(f32[8,64,512]{1,2,0:T(8,128)} %gather_fusion.3) | data formatting | bytes 2097152 | tf_op jit(solution)/shard_map/jit(_take)/gather | solution.py:89
  139.5 9.7 %fusion.26 = f32[64,2,512]{2,0,1:T(8,128)S(1)} fusion(f32[2,512]{1,0:T(2,128)S(1)} %copy-done.13, f32[2,4,512]{2,1,0:T(4,128)S(1)} %copy-done.5, f32[2,512]{1,0:T(2,128)S(1)} %copy-done.11, f32[2,4,512]{2,1,0:T(4,128)S(1)} %copy-done.7, f32[2,512]{1,0:T(2,128)S(1)} %copy-done.9, f32[2,4,512]{2,1,0:T(4,128)S(1)} %bitcast.184, ...), kind=kOutput, calls=%fused_computation.38 | convolution fusion | flops 1629749248 | bytes 1372168 | tf_op jit(solution)/shard_map/clnp,lnpq->clq/dot_general | solution.py:90
  150.5 39.2 %psum.7 = f32[64]{0:T(128)S(1)} all-reduce(f32[64]{0:T(128)S(1)} %get-tuple-element.109), channel_id=1, replica_groups=mesh['leaf'=16,'sub'=2] {'leaf','sub'}, use_global_device_ids=true, to_apply=%region_5.8 | all-reduce | flops 64 | bytes 512 | tf_op jit(solution)/shard_map/psum | solution.py:149
  199.2 10.4 %reduce-scatter.5.cloned.1.call-done = f32[32,256]{1,0:T(8,128)} async-done(((f32[64,256]{1,0:T(8,128)}), f32[32,256]{1,0:T(8,128)}) %reduce-scatter.5.cloned.1.call-update) | async-done | bytes 32784 | tf_op jit(solution)/shard_map/reduce_scatter | solution.py:66
  210.3 2.4 collective-permute-start.25
  214.0 5.3 %collective-permute-start.19 = (f32[32,256]{1,0:T(8,128)}, f32[32,256]{1,0:T(8,128)S(1)}, u32[]{:S(2)}, u32[]{:S(2)}) collective-permute-start(f32[32,256]{1,0:T(8,128)} %reduce-scatter.5.cloned.1.call-done), channel_id=1, source_target_pairs={{6,0},{8,2},{10,4},{12,6},{14,8},{16,10},{18,12},{20,14},{22,16},{... | collective-permute-start | bytes 98312 | tf_op jit(solution)/shard_map/ppermute | solution.py:15
  220.6 4.5 %collective-permute-start.20 = (f32[32,256]{1,0:T(8,128)}, f32[32,256]{1,0:T(8,128)S(1)}, u32[]{:S(2)}, u32[]{:S(2)}) collective-permute-start(f32[32,256]{1,0:T(8,128)} %reduce-scatter.5.cloned.1.call-done), channel_id=1, source_target_pairs={{8,0},{10,2},{12,4},{14,6},{16,8},{18,10},{20,12},{22,14},{24,16},... | collective-permute-start | bytes 98312 | tf_op jit(solution)/shard_map/ppermute | solution.py:15
  226.4 2.6 collective-permute-start.21
  230.4 1.8 collective-permute-start.22
  233.5 2.4 collective-permute-start.23
  235.9 4.2 %collective-permute-done.23 = f32[32,256]{1,0:T(8,128)S(1)} collective-permute-done((f32[32,256]{1,0:T(8,128)}, f32[32,256]{1,0:T(8,128)S(1)}, u32[]{:S(2)}, u32[]{:S(2)}) %collective-permute-start.23) | collective-permute-done | bytes 32800 | tf_op jit(solution)/shard_map/ppermute | solution.py:15
  240.2 42.2 %while.21 = (s32[]{:T(128)}, f32[32,256]{1,0:T(8,128)S(1)}, s32[]{:T(128)}, s32[8]{0:T(128)}, f32[8,32,256]{2,1,0:T(8,128)S(1)}, /*index=5*/f32[8,256,256]{2,1,0:T(8,128)}, s32[]{:T(128)}, s32[]{:T(128)}, s32[]{:T(128)}) while((s32[]{:T(128)}, f32[32,256]{1,0:T(8,128)S(1)}, s32[]{:T(128)}, s32[8]{0:T(128)}, f32[8,32,256]{2,1,0:T(8,128)S(1)}, ...), condition=%wide.region_8.11_spmd, body=%wide.region_7.10_spmd.sunk | while | flops 25174024 | bytes 360637 | solution.py:50
  282.4 8.1 %all_gather.7 = f32[64,256]{1,0:T(8,128)S(1)} all-gather(f32[32,256]{1,0:T(8,128)S(1)} %get-tuple-element.74), channel_id=1, replica_groups=mesh['leaf'=16,'sub'=2] {'sub'}, dimensions={0}, use_global_device_ids=true | all-gather | bytes 98304 | tf_op jit(solution)/shard_map/all_gather | solution.py:69
  294.2 9.7 %fusion.27 = f32[64,2,512]{2,0,1:T(8,128)S(1)} fusion(f32[2,512]{1,0:T(2,128)S(1)} %copy-done.14, f32[2,4,512]{2,1,0:T(4,128)S(1)} %copy-done.6, f32[2,512]{1,0:T(2,128)S(1)} %copy-done.12, f32[2,4,512]{2,1,0:T(4,128)S(1)} %copy-done.8, f32[2,512]{1,0:T(2,128)S(1)} %copy-done.10, f32[2,4,512]{2,1,0:T(4,128)S(1)} %bitcast.185, ...), kind=kOutput, calls=%fused_computation.39 | convolution fusion | flops 1629749248 | bytes 1372168 | tf_op jit(solution)/shard_map/clnp,lnpq->clq/dot_general | solution.py:90
  305.2 3.3 %scatter_custom_fusion = f32[64,1024]{0,1:T(8,128)S(1)} fusion(s32[1024]{0:T(1024)} %get-tuple-element.108, f32[1024,64]{1,0:T(8,128)S(1)} %copy.49, f32[]{:T(128)} %constant.109.clone.1), kind=kCustom, calls=%fused_computation.71 | custom fusion | bytes 262656 | tf_op jit(solution)/shard_map/scatter | solution.py:163
  (182 shorter events, 96.3 us)
Async XLA Ops:
  6.5 44.5 %copy-start = (f32[4,256,256]{2,1,0:T(8,128)S(1)}, f32[4,256,256]{2,1,0:T(8,128)}, u32[]{:S(2)}) copy-start(f32[4,256,256]{2,1,0:T(8,128)} %param.26) | copy-start | bytes 3145732
  6.5 38.6 %reduce-scatter.3.cloned.1.call-start = ((), (), s32[]{:S(2)}) async-start(), calls=%async_computation.2 | async-start | bytes 98304 | tf_op jit(solution)/shard_map/reduce_scatter | solution.py:66
  13.1 16.4 %copy-start.19 = (s32[1,8]{1,0:T(1,128)S(1)}, s32[1,8]{1,0:T(1,128)}, u32[]{:S(2)}) copy-start(s32[1,8]{1,0:T(1,128)} %param.23) | copy-start | bytes 100
  13.1 17.0 %copy-start.17 = (s32[2,4]{1,0:T(2,128)S(1)}, s32[2,4]{1,0:T(2,128)}, u32[]{:S(2)}) copy-start(s32[2,4]{1,0:T(2,128)} %param.21) | copy-start | bytes 100
  15.2 28.4 %collective-permute-start.5 = (f32[2,64,256]{2,1,0:T(8,128)S(1)}, f32[2,64,256]{2,1,0:T(8,128)S(1)}, u32[]{:S(2)}, u32[]{:S(2)}) collective-permute-start(f32[2,64,256]{2,1,0:T(8,128)S(1)} %fusion.58), channel_id=1, source_target_pairs={{1,0},{2,1},{3,2},{4,3},{5,4},{6,5},{7,6},{8,7},{9,8},{10,9},{11,1... | collective-permute-start | bytes 393224 | tf_op jit(solution)/shard_map/ppermute | solution.py:15
  15.9 27.7 %collective-permute-start.4 = (f32[2,64,256]{2,1,0:T(8,128)S(1)}, f32[2,64,256]{2,1,0:T(8,128)S(1)}, u32[]{:S(2)}, u32[]{:S(2)}) collective-permute-start(f32[2,64,256]{2,1,0:T(8,128)S(1)} %fusion.58), channel_id=1, source_target_pairs={{31,0},{0,1},{1,2},{2,3},{3,4},{4,5},{5,6},{6,7},{7,8},{8,9},{9,10... | collective-permute-start | bytes 393224 | tf_op jit(solution)/shard_map/ppermute | solution.py:15
  22.7 13.9 %collective-permute-start.1 = (f32[3,1024]{0,1:T(8,128)S(1)}, f32[3,1024]{0,1:T(8,128)}, u32[]{:S(2)}, u32[]{:S(2)}) collective-permute-start(f32[3,1024]{0,1:T(8,128)S(1)} %bitcast.164), channel_id=1, source_target_pairs={{1,0},{2,1},{3,2},{4,3},{5,4},{6,5},{7,6},{8,7},{9,8},{10,9},{11,1... | collective-permute-start | bytes 36872 | tf_op jit(solution)/shard_map/ppermute | solution.py:15
  22.8 16.8 %collective-permute-start = (f32[3,1024]{0,1:T(8,128)S(1)}, f32[3,1024]{0,1:T(8,128)}, u32[]{:S(2)}, u32[]{:S(2)}) collective-permute-start(f32[3,1024]{0,1:T(8,128)S(1)} %bitcast.165), channel_id=1, source_target_pairs={{31,0},{0,1},{1,2},{2,3},{3,4},{4,5},{5,6},{6,7},{7,8},{8,9},{9,10... | collective-permute-start | bytes 36872 | tf_op jit(solution)/shard_map/ppermute | solution.py:15
  25.6 184.0 %reduce-scatter.5.cloned.1.call-start = ((), (), s32[]{:S(2)}) async-start(), calls=%async_computation.3 | async-start | bytes 98304 | tf_op jit(solution)/shard_map/reduce_scatter | solution.py:66
  25.6 104.6 %collective-permute-start.3 = (f32[64,1024]{0,1:T(8,128)}, f32[64,1024]{0,1:T(8,128)}, u32[]{:S(2)}, u32[]{:S(2)}) collective-permute-start(f32[64,1024]{0,1:T(8,128)} %bitcast.171), channel_id=1, source_target_pairs={{1,0},{2,1},{3,2},{4,3},{5,4},{6,5},{7,6},{8,7},{9,8},{10,9},{11,1... | collective-permute-start | bytes 786440 | tf_op jit(solution)/shard_map/ppermute | solution.py:15
  36.6 93.6 %collective-permute-start.2 = (f32[64,1024]{0,1:T(8,128)}, f32[64,1024]{0,1:T(8,128)}, u32[]{:S(2)}, u32[]{:S(2)}) collective-permute-start(f32[64,1024]{0,1:T(8,128)} %bitcast.172), channel_id=1, source_target_pairs={{31,0},{0,1},{1,2},{2,3},{3,4},{4,5},{5,6},{6,7},{7,8},{8,9},{9,10... | collective-permute-start | bytes 786440 | tf_op jit(solution)/shard_map/ppermute | solution.py:15
  45.1 9.7 %collective-permute-start.6 = (f32[32,256]{1,0:T(8,128)}, f32[32,256]{1,0:T(8,128)S(1)}, u32[]{:S(2)}, u32[]{:S(2)}) collective-permute-start(f32[32,256]{1,0:T(8,128)} %reduce-scatter.3.cloned.1.call-done), channel_id=1, source_target_pairs={{4,0},{6,2},{8,4},{10,6},{12,8},{14,10},{16,12},{18,14},{20,16},{2... | collective-permute-start | bytes 98312 | tf_op jit(solution)/shard_map/ppermute | solution.py:15
  51.8 78.5 %copy-start.3 = (f32[1024,64]{1,0:T(8,128)S(1)}, f32[1024,64]{1,0:T(8,128)}, u32[]{:S(2)}) copy-start(f32[1024,64]{1,0:T(8,128)} %gather_fusion.2) | copy-start | bytes 786436
  51.8 34.6 %collective-permute-start.13 = (f32[32,256]{1,0:T(8,128)}, f32[32,256]{1,0:T(8,128)S(1)}, u32[]{:S(2)}, u32[]{:S(2)}) collective-permute-start(f32[32,256]{1,0:T(8,128)} %reduce-scatter.3.cloned.1.call-done), channel_id=1, source_target_pairs={{22,0},{24,2},{26,4},{28,6},{30,8},{0,10},{2,12},{4,14},{6,16},{8,... | collective-permute-start | bytes 98312 | tf_op jit(solution)/shard_map/ppermute | solution.py:15
  53.6 32.9 %collective-permute-start.12 = (f32[32,256]{1,0:T(8,128)}, f32[32,256]{1,0:T(8,128)S(1)}, u32[]{:S(2)}, u32[]{:S(2)}) collective-permute-start(f32[32,256]{1,0:T(8,128)} %reduce-scatter.3.cloned.1.call-done), channel_id=1, source_target_pairs={{24,0},{26,2},{28,4},{30,6},{0,8},{2,10},{4,12},{6,14},{8,16},{10,... | collective-permute-start | bytes 98312 | tf_op jit(solution)/shard_map/ppermute | solution.py:15
  54.9 12.3 %collective-permute-start.7 = (f32[32,256]{1,0:T(8,128)}, f32[32,256]{1,0:T(8,128)S(1)}, u32[]{:S(2)}, u32[]{:S(2)}) collective-permute-start(f32[32,256]{1,0:T(8,128)} %reduce-scatter.3.cloned.1.call-done), channel_id=1, source_target_pairs={{6,0},{8,2},{10,4},{12,6},{14,8},{16,10},{18,12},{20,14},{22,16},{... | collective-permute-start | bytes 98312 | tf_op jit(solution)/shard_map/ppermute | solution.py:15
  67.1 3.4 %collective-permute-start.8 = (f32[32,256]{1,0:T(8,128)}, f32[32,256]{1,0:T(8,128)S(1)}, u32[]{:S(2)}, u32[]{:S(2)}) collective-permute-start(f32[32,256]{1,0:T(8,128)} %reduce-scatter.3.cloned.1.call-done), channel_id=1, source_target_pairs={{8,0},{10,2},{12,4},{14,6},{16,8},{18,10},{20,12},{22,14},{24,16},... | collective-permute-start | bytes 98312 | tf_op jit(solution)/shard_map/ppermute | solution.py:15
  70.6 6.4 %collective-permute-start.9 = (f32[32,256]{1,0:T(8,128)}, f32[32,256]{1,0:T(8,128)S(1)}, u32[]{:S(2)}, u32[]{:S(2)}) collective-permute-start(f32[32,256]{1,0:T(8,128)} %reduce-scatter.3.cloned.1.call-done), channel_id=1, source_target_pairs={{10,0},{12,2},{14,4},{16,6},{18,8},{20,10},{22,12},{24,14},{26,16}... | collective-permute-start | bytes 98312 | tf_op jit(solution)/shard_map/ppermute | solution.py:15
  77.0 3.3 %collective-permute-start.10 = (f32[32,256]{1,0:T(8,128)}, f32[32,256]{1,0:T(8,128)S(1)}, u32[]{:S(2)}, u32[]{:S(2)}) collective-permute-start(f32[32,256]{1,0:T(8,128)} %reduce-scatter.3.cloned.1.call-done), channel_id=1, source_target_pairs={{28,0},{30,2},{0,4},{2,6},{4,8},{6,10},{8,12},{10,14},{12,16},{14,... | collective-permute-start | bytes 98312 | tf_op jit(solution)/shard_map/ppermute | solution.py:15
  80.3 6.1 %collective-permute-start.11 = (f32[32,256]{1,0:T(8,128)}, f32[32,256]{1,0:T(8,128)S(1)}, u32[]{:S(2)}, u32[]{:S(2)}) collective-permute-start(f32[32,256]{1,0:T(8,128)} %reduce-scatter.3.cloned.1.call-done), channel_id=1, source_target_pairs={{26,0},{28,2},{30,4},{0,6},{2,8},{4,10},{6,12},{8,14},{10,16},{12,... | collective-permute-start | bytes 98312 | tf_op jit(solution)/shard_map/ppermute | solution.py:15
  190.5 6.3 %collective-permute-start.17 = (f32[2,64,256]{2,1,0:T(8,128)S(1)}, f32[2,64,256]{2,1,0:T(8,128)S(1)}, u32[]{:S(2)}, u32[]{:S(2)}) collective-permute-start(f32[2,64,256]{2,1,0:T(8,128)S(1)} %fusion.41), channel_id=1, source_target_pairs={{1,0},{2,1},{3,2},{4,3},{5,4},{6,5},{7,6},{8,7},{9,8},{10,9},{11,1... | collective-permute-start | bytes 393224 | tf_op jit(solution)/shard_map/ppermute | solution.py:15
  191.7 5.1 %collective-permute-start.16 = (f32[2,64,256]{2,1,0:T(8,128)S(1)}, f32[2,64,256]{2,1,0:T(8,128)}, u32[]{:S(2)}, u32[]{:S(2)}) collective-permute-start(f32[2,64,256]{2,1,0:T(8,128)S(1)} %fusion.41), channel_id=1, source_target_pairs={{31,0},{0,1},{1,2},{2,3},{3,4},{4,5},{5,6},{6,7},{7,8},{8,9},{9,10... | collective-permute-start | bytes 393224 | tf_op jit(solution)/shard_map/ppermute | solution.py:15
  194.0 97.1 %collective-permute-start.15 = (f32[64,1024]{1,0:T(8,128)}, f32[64,1024]{1,0:T(8,128)}, u32[]{:S(2)}, u32[]{:S(2)}) collective-permute-start(f32[64,1024]{1,0:T(8,128)} %broadcast_multiply_fusion), channel_id=1, source_target_pairs={{1,0},{2,1},{3,2},{4,3},{5,4},{6,5},{7,6},{8,7},{9,8},{10,9},{11,1... | collective-permute-start | bytes 786440 | tf_op jit(solution)/shard_map/ppermute | solution.py:15
  194.0 97.1 %collective-permute-start.14 = (f32[64,1024]{1,0:T(8,128)}, f32[64,1024]{1,0:T(8,128)}, u32[]{:S(2)}, u32[]{:S(2)}) collective-permute-start(f32[64,1024]{1,0:T(8,128)} %broadcast_multiply_fusion), channel_id=1, source_target_pairs={{31,0},{0,1},{1,2},{2,3},{3,4},{4,5},{5,6},{6,7},{7,8},{8,9},{9,10... | collective-permute-start | bytes 786440 | tf_op jit(solution)/shard_map/ppermute | solution.py:15
  209.6 4.4 %collective-permute-start.18 = (f32[32,256]{1,0:T(8,128)}, f32[32,256]{1,0:T(8,128)S(1)}, u32[]{:S(2)}, u32[]{:S(2)}) collective-permute-start(f32[32,256]{1,0:T(8,128)} %reduce-scatter.5.cloned.1.call-done), channel_id=1, source_target_pairs={{4,0},{6,2},{8,4},{10,6},{12,8},{14,10},{16,12},{18,14},{20,16},{2... | collective-permute-start | bytes 98312 | tf_op jit(solution)/shard_map/ppermute | solution.py:15
  210.3 29.8 %collective-permute-start.25 = (f32[32,256]{1,0:T(8,128)}, f32[32,256]{1,0:T(8,128)S(1)}, u32[]{:S(2)}, u32[]{:S(2)}) collective-permute-start(f32[32,256]{1,0:T(8,128)} %reduce-scatter.5.cloned.1.call-done), channel_id=1, source_target_pairs={{22,0},{24,2},{26,4},{28,6},{30,8},{0,10},{2,12},{4,14},{6,16},{8,... | collective-permute-start | bytes 98312 | tf_op jit(solution)/shard_map/ppermute | solution.py:15
  212.8 27.4 %collective-permute-start.24 = (f32[32,256]{1,0:T(8,128)}, f32[32,256]{1,0:T(8,128)S(1)}, u32[]{:S(2)}, u32[]{:S(2)}) collective-permute-start(f32[32,256]{1,0:T(8,128)} %reduce-scatter.5.cloned.1.call-done), channel_id=1, source_target_pairs={{24,0},{26,2},{28,4},{30,6},{0,8},{2,10},{4,12},{6,14},{8,16},{10,... | collective-permute-start | bytes 98312 | tf_op jit(solution)/shard_map/ppermute | solution.py:15
  214.0 6.6 %collective-permute-start.19 = (f32[32,256]{1,0:T(8,128)}, f32[32,256]{1,0:T(8,128)S(1)}, u32[]{:S(2)}, u32[]{:S(2)}) collective-permute-start(f32[32,256]{1,0:T(8,128)} %reduce-scatter.5.cloned.1.call-done), channel_id=1, source_target_pairs={{6,0},{8,2},{10,4},{12,6},{14,8},{16,10},{18,12},{20,14},{22,16},{... | collective-permute-start | bytes 98312 | tf_op jit(solution)/shard_map/ppermute | solution.py:15
  220.6 5.8 %collective-permute-start.20 = (f32[32,256]{1,0:T(8,128)}, f32[32,256]{1,0:T(8,128)S(1)}, u32[]{:S(2)}, u32[]{:S(2)}) collective-permute-start(f32[32,256]{1,0:T(8,128)} %reduce-scatter.5.cloned.1.call-done), channel_id=1, source_target_pairs={{8,0},{10,2},{12,4},{14,6},{16,8},{18,10},{20,12},{22,14},{24,16},... | collective-permute-start | bytes 98312 | tf_op jit(solution)/shard_map/ppermute | solution.py:15
  226.4 4.0 %collective-permute-start.21 = (f32[32,256]{1,0:T(8,128)}, f32[32,256]{1,0:T(8,128)S(1)}, u32[]{:S(2)}, u32[]{:S(2)}) collective-permute-start(f32[32,256]{1,0:T(8,128)} %reduce-scatter.5.cloned.1.call-done), channel_id=1, source_target_pairs={{10,0},{12,2},{14,4},{16,6},{18,8},{20,10},{22,12},{24,14},{26,16}... | collective-permute-start | bytes 98312 | tf_op jit(solution)/shard_map/ppermute | solution.py:15
  230.4 3.2 %collective-permute-start.22 = (f32[32,256]{1,0:T(8,128)}, f32[32,256]{1,0:T(8,128)S(1)}, u32[]{:S(2)}, u32[]{:S(2)}) collective-permute-start(f32[32,256]{1,0:T(8,128)} %reduce-scatter.5.cloned.1.call-done), channel_id=1, source_target_pairs={{28,0},{30,2},{0,4},{2,6},{4,8},{6,10},{8,12},{10,14},{12,16},{14,... | collective-permute-start | bytes 98312 | tf_op jit(solution)/shard_map/ppermute | solution.py:15
  233.5 6.6 %collective-permute-start.23 = (f32[32,256]{1,0:T(8,128)}, f32[32,256]{1,0:T(8,128)S(1)}, u32[]{:S(2)}, u32[]{:S(2)}) collective-permute-start(f32[32,256]{1,0:T(8,128)} %reduce-scatter.5.cloned.1.call-done), channel_id=1, source_target_pairs={{26,0},{28,2},{30,4},{0,6},{2,8},{4,10},{6,12},{8,14},{10,16},{12,... | collective-permute-start | bytes 98312 | tf_op jit(solution)/shard_map/ppermute | solution.py:15
  (17 other events, 66.7 us)
Sparse Core Ops, SparseCore 0:
  25.7 16.0 reduce-scatter.2
  196.9 12.6 reduce-scatter.4
where the time goes:
time: 318 us; the launch traced here: 316 us
  starting transfers between devices  59.5 us (19%)
  local copies, waits for them, and re-layouts  57 us (18%)
  blocking collectives  51.2 us (16%)
  matrix products  48.7 us (15%)
  loops' own time  41 us (13%)
  waiting for transfers between devices  31.1 us (10%)
  other arithmetic  13.9 us (4%)
  between operations  13.9 us (4%)
    ppermute x26, starting transfers between devices, from_behind(): return lax.ppermute(block, axis, route)  59.5 us
    another operation x2, loops' own time, couple_chips(): return lax.fori_loop(0, used_count, add_slot, start_value)  41 us
    psum x1, blocking collectives, on_device(): lax.psum(jnp.sum(first_pass * first_pass, axis=1), ('leaf', 'sub'))  39.2 us
    ppermute x26, waiting for transfers between devices, from_behind(): return lax.ppermute(block, axis, route)  20.7 us
    dynamic_slice x16, local copies, waits for them, and re-layouts, add_slot(): source = stacked[slot_place[slot_index]]  20.5 us
    dot_general x2, matrix products, apply_matrix(): jnp.einsum('clnp,lnpq->clq', source_values, kernels, precision=highest)  19.5 us
    dot_general x16, matrix products, add_slot(): jnp.dot(source, far_chip_blocks[slot_index], precision=highest, preferred...  19.2 us
    all_gather x2, blocking collectives, chip_level(): coupled = lax.all_gather(coupled_half, 'sub', axis=0, tiled=True)  11.9 us
  transfers between devices with their start and end apart: 28, of which 11 were waited for; matrix products, arithmetic and copies ran while one was open for 22% of the time, Pallas kernels for 0%

commit v1 on v0

--- a/solution.py
+++ b/solution.py
@@ -146,7 +146,8 @@
         far_chip_blocks,
         leaf_total,
     )
-    squares = lax.psum(jnp.sum(first_pass * first_pass, axis=1), ("leaf", "sub"))
+    half = lax.psum(jnp.sum(first_pass * first_pass, axis=1), "sub")
+    squares = lax.psum(half, "leaf")
     column_scale = lax.rsqrt(squares / point_total + epsilon)
     second = apply_matrix(
         first_pass * column_scale[:, None],

time: 318 us -> 317 us (level)
  blocking collectives: 51.2 us -> 39.4 us
  starting transfers between devices: 59.5 us -> 65.8 us
  loops' own time: 41 us -> 44.2 us
    psum x1 -> x2, blocking collectives: 39.2 us -> 27.4 us  [the longest x1 25 us: on_device(): squares = lax.psum(half, 'leaf')]
    ppermute x26, starting transfers between devices: 59.5 us -> 65.8 us  [from_behind(): return lax.ppermute(block, axis, route)]
where the time goes in v1:
time: 317 us; the launch traced here: 315 us
  starting transfers between devices  65.8 us (21%)
  local copies, waits for them, and re-layouts  56.2 us (18%)
  matrix products  48.7 us (15%)
  loops' own time  44.2 us (14%)
  blocking collectives  39.4 us (12%)
  waiting for transfers between devices  32.8 us (10%)
  between operations  13.9 us (4%)
  other arithmetic  13.7 us (4%)
    ppermute x26, starting transfers between devices, from_behind(): return lax.ppermute(block, axis, route)  65.8 us
    another operation x2, loops' own time, couple_chips(): return lax.fori_loop(0, used_count, add_slot, start_value)  44.2 us
    psum x1, blocking collectives, on_device(): squares = lax.psum(half, 'leaf')  25 us
    ppermute x26, waiting for transfers between devices, from_behind(): return lax.ppermute(block, axis, route)  20.6 us
    dynamic_slice x16, local copies, waits for them, and re-layouts, add_slot(): source = stacked[slot_place[slot_index]]  19.7 us
    dot_general x2, matrix products, apply_matrix(): jnp.einsum('clnp,lnpq->clq', source_values, kernels, precision=highest)  19.5 us
    dot_general x16, matrix products, add_slot(): jnp.dot(source, far_chip_blocks[slot_index], precision=highest, preferred...  19.2 us
    reduce_scatter x2, waiting for transfers between devices, chip_level(): halves = lax.psum_scatter(upward, 'sub', scatter_dimension=0, tiled=True)  12.2 us
  transfers between devices with their start and end apart: 28, of which 11 were waited for; matrix products, arithmetic and copies ran while one was open for 22% of the time, Pallas kernels for 0%

profile of v1, /device:TPU:5, one launch (start us, length us, event | category | flops | bytes accessed | tf_op | source)
XLA Modules:
  0.0 314.7 jit_solution(10121775175738408827)
XLA Ops:
  9.1 4.0 %gather_fusion.2 = f32[1024,64]{1,0:T(8,128)} fusion(f32[64,1024]{0,1:T(8,128)S(1)} %copy.43, s32[1024]{0:T(1024)S(1)} %get-tuple-element.107), kind=kCustom, calls=%fused_computation.6 | custom fusion | bytes 528384 | tf_op jit(solution)/shard_map/gather | solution.py:129
  13.2 2.1 fusion.58
  18.9 3.8 %gather_fusion = f32[1024,3]{1,0:T(8,128)S(1)} fusion(f32[3,1024]{0,1:T(8,128)} %copy.39, s32[1024]{0:T(1024)S(1)} %get-tuple-element.107), kind=kCustom, calls=%fused_computation.4 | custom fusion | bytes 28672 | tf_op jit(solution)/shard_map/gather | solution.py:130
  37.7 1.8 copy.42
  45.1 5.9 %collective-permute-start.6 = (f32[32,256]{1,0:T(8,128)}, f32[32,256]{1,0:T(8,128)S(1)}, u32[]{:S(2)}, u32[]{:S(2)}) collective-permute-start(f32[32,256]{1,0:T(8,128)} %reduce-scatter.3.cloned.1.call-done), channel_id=1, source_target_pairs={{4,0},{6,2},{8,4},{10,6},{12,8},{14,10},{16,12},{18,14},{20,16},{2... | collective-permute-start | bytes 98312 | tf_op jit(solution)/shard_map/ppermute | solution.py:15
  54.8 10.9 %collective-permute-start.7 = (f32[32,256]{1,0:T(8,128)}, f32[32,256]{1,0:T(8,128)S(1)}, u32[]{:S(2)}, u32[]{:S(2)}) collective-permute-start(f32[32,256]{1,0:T(8,128)} %reduce-scatter.3.cloned.1.call-done), channel_id=1, source_target_pairs={{6,0},{8,2},{10,4},{12,6},{14,8},{16,10},{18,12},{20,14},{22,16},{... | collective-permute-start | bytes 98312 | tf_op jit(solution)/shard_map/ppermute | solution.py:15
  67.3 3.2 %collective-permute-done.8 = f32[32,256]{1,0:T(8,128)S(1)} collective-permute-done((f32[32,256]{1,0:T(8,128)}, f32[32,256]{1,0:T(8,128)S(1)}, u32[]{:S(2)}, u32[]{:S(2)}) %collective-permute-start.8) | collective-permute-done | bytes 32800 | tf_op jit(solution)/shard_map/ppermute | solution.py:15
  70.5 5.1 %collective-permute-start.9 = (f32[32,256]{1,0:T(8,128)}, f32[32,256]{1,0:T(8,128)S(1)}, u32[]{:S(2)}, u32[]{:S(2)}) collective-permute-start(f32[32,256]{1,0:T(8,128)} %reduce-scatter.3.cloned.1.call-done), channel_id=1, source_target_pairs={{10,0},{12,2},{14,4},{16,6},{18,8},{20,10},{22,12},{24,14},{26,16}... | collective-permute-start | bytes 98312 | tf_op jit(solution)/shard_map/ppermute | solution.py:15
  77.0 1.8 collective-permute-start.10
  80.3 2.5 collective-permute-start.11
  82.7 3.7 %collective-permute-done.11 = f32[32,256]{1,0:T(8,128)S(1)} collective-permute-done((f32[32,256]{1,0:T(8,128)}, f32[32,256]{1,0:T(8,128)S(1)}, u32[]{:S(2)}, u32[]{:S(2)}) %collective-permute-start.11) | collective-permute-done | bytes 32800 | tf_op jit(solution)/shard_map/ppermute | solution.py:15
  87.1 41.1 %while.20 = (s32[]{:T(128)}, f32[32,256]{1,0:T(8,128)S(1)}, s32[]{:T(128)}, s32[8]{0:T(128)}, f32[8,32,256]{2,1,0:T(8,128)}, /*index=5*/f32[8,256,256]{2,1,0:T(8,128)}, s32[]{:T(128)}, s32[]{:T(128)}, s32[]{:T(128)}) while((s32[]{:T(128)}, f32[32,256]{1,0:T(8,128)S(1)}, s32[]{:T(128)}, s32[8]{0:T(128)}, f32[8,32,256]{2,1,0:T(8,128)}, ...), condition=%wide.region_3.6_spmd, body=%wide.region_2.5_spmd.sunk | while | flops 25174024 | bytes 360637 | solution.py:50
  128.3 3.8 %all_gather.6 = f32[64,256]{1,0:T(8,128)S(1)} all-gather(f32[32,256]{1,0:T(8,128)S(1)} %get-tuple-element.73), channel_id=1, replica_groups=mesh['leaf'=16,'sub'=2] {'sub'}, dimensions={0}, use_global_device_ids=true | all-gather | bytes 98304 | tf_op jit(solution)/shard_map/all_gather | solution.py:69
  132.7 2.4 pad_maximum_fusion
  135.2 3.6 %gather_fusion.3 = f32[8,64,512]{1,2,0:T(8,128)} fusion(f32[64,6,512]{0,2,1:T(8,128)} %bitcast.168, s32[1024]{0:T(1024)} %pad_clamp_fusion.1), kind=kCustom, calls=%fused_computation.clone | custom fusion | bytes 2097184 | tf_op jit(solution)/shard_map/jit(_take)/gather | solution.py:89
  138.8 3.2 %copy.44 = f32[8,64,512]{2,1,0:T(8,128)} copy(f32[8,64,512]{1,2,0:T(8,128)} %gather_fusion.3) | data formatting | bytes 2097152 | tf_op jit(solution)/shard_map/jit(_take)/gather | solution.py:89
  142.0 9.7 %fusion.26 = f32[64,2,512]{2,0,1:T(8,128)S(1)} fusion(f32[2,512]{1,0:T(2,128)S(1)} %copy-done.13, f32[2,4,512]{2,1,0:T(4,128)S(1)} %copy-done.5, f32[2,512]{1,0:T(2,128)S(1)} %copy-done.11, f32[2,4,512]{2,1,0:T(4,128)S(1)} %copy-done.7, f32[2,512]{1,0:T(2,128)S(1)} %copy-done.9, f32[2,4,512]{2,1,0:T(4,128)S(1)} %bitcast.184, ...), kind=kOutput, calls=%fused_computation.38 | convolution fusion | flops 1629749248 | bytes 1372168 | tf_op jit(solution)/shard_map/clnp,lnpq->clq/dot_general | solution.py:90
  153.0 2.5 psum.14
  155.4 25.0 %psum.15 = f32[64]{0:T(128)S(1)} all-reduce(f32[64]{0:T(128)S(1)} %psum.14), channel_id=1, replica_groups=mesh['leaf'=16,'sub'=2] {'leaf'}, use_global_device_ids=true, to_apply=%region_6.9 | all-reduce | flops 64 | bytes 512 | tf_op jit(solution)/shard_map/psum | solution.py:150
  181.2 7.2 %collective-permute-start.17 = (f32[2,64,256]{2,1,0:T(8,128)S(1)}, f32[2,64,256]{2,1,0:T(8,128)S(1)}, u32[]{:S(2)}, u32[]{:S(2)}) collective-permute-start(f32[2,64,256]{2,1,0:T(8,128)S(1)} %fusion.41), channel_id=1, source_target_pairs={{1,0},{2,1},{3,2},{4,3},{5,4},{6,5},{7,6},{8,7},{9,8},{10,9},{11,1... | collective-permute-start | bytes 393224 | tf_op jit(solution)/shard_map/ppermute | solution.py:15
  196.0 12.2 %reduce-scatter.5.cloned.1.call-done = f32[32,256]{1,0:T(8,128)} async-done(((f32[64,256]{1,0:T(8,128)}), f32[32,256]{1,0:T(8,128)}) %reduce-scatter.5.cloned.1.call-update) | async-done | bytes 32784 | tf_op jit(solution)/shard_map/reduce_scatter | solution.py:66
  208.9 2.4 collective-permute-start.25
  212.6 5.2 %collective-permute-start.19 = (f32[32,256]{1,0:T(8,128)}, f32[32,256]{1,0:T(8,128)S(1)}, u32[]{:S(2)}, u32[]{:S(2)}) collective-permute-start(f32[32,256]{1,0:T(8,128)} %reduce-scatter.5.cloned.1.call-done), channel_id=1, source_target_pairs={{6,0},{8,2},{10,4},{12,6},{14,8},{16,10},{18,12},{20,14},{22,16},{... | collective-permute-start | bytes 98312 | tf_op jit(solution)/shard_map/ppermute | solution.py:15
  219.2 4.5 %collective-permute-start.20 = (f32[32,256]{1,0:T(8,128)}, f32[32,256]{1,0:T(8,128)S(1)}, u32[]{:S(2)}, u32[]{:S(2)}) collective-permute-start(f32[32,256]{1,0:T(8,128)} %reduce-scatter.5.cloned.1.call-done), channel_id=1, source_target_pairs={{8,0},{10,2},{12,4},{14,6},{16,8},{18,10},{20,12},{22,14},{24,16},... | collective-permute-start | bytes 98312 | tf_op jit(solution)/shard_map/ppermute | solution.py:15
  225.0 2.6 collective-permute-start.21
  229.0 1.8 collective-permute-start.22
  232.1 2.4 collective-permute-start.23
  234.6 4.2 %collective-permute-done.23 = f32[32,256]{1,0:T(8,128)S(1)} collective-permute-done((f32[32,256]{1,0:T(8,128)}, f32[32,256]{1,0:T(8,128)S(1)}, u32[]{:S(2)}, u32[]{:S(2)}) %collective-permute-start.23) | collective-permute-done | bytes 32800 | tf_op jit(solution)/shard_map/ppermute | solution.py:15
  238.8 42.0 %while.21 = (s32[]{:T(128)}, f32[32,256]{1,0:T(8,128)S(1)}, s32[]{:T(128)}, s32[8]{0:T(128)}, f32[8,32,256]{2,1,0:T(8,128)S(1)}, /*index=5*/f32[8,256,256]{2,1,0:T(8,128)}, s32[]{:T(128)}, s32[]{:T(128)}, s32[]{:T(128)}) while((s32[]{:T(128)}, f32[32,256]{1,0:T(8,128)S(1)}, s32[]{:T(128)}, s32[8]{0:T(128)}, f32[8,32,256]{2,1,0:T(8,128)S(1)}, ...), condition=%wide.region_9.12_spmd, body=%wide.region_8.11_spmd.sunk | while | flops 25174024 | bytes 360637 | solution.py:50
  280.8 8.1 %all_gather.7 = f32[64,256]{1,0:T(8,128)S(1)} all-gather(f32[32,256]{1,0:T(8,128)S(1)} %get-tuple-element.74), channel_id=1, replica_groups=mesh['leaf'=16,'sub'=2] {'sub'}, dimensions={0}, use_global_device_ids=true | all-gather | bytes 98304 | tf_op jit(solution)/shard_map/all_gather | solution.py:69
  292.6 9.7 %fusion.27 = f32[64,2,512]{2,0,1:T(8,128)S(1)} fusion(f32[2,512]{1,0:T(2,128)S(1)} %copy-done.14, f32[2,4,512]{2,1,0:T(4,128)S(1)} %copy-done.6, f32[2,512]{1,0:T(2,128)S(1)} %copy-done.12, f32[2,4,512]{2,1,0:T(4,128)S(1)} %copy-done.8, f32[2,512]{1,0:T(2,128)S(1)} %copy-done.10, f32[2,4,512]{2,1,0:T(4,128)S(1)} %bitcast.185, ...), kind=kOutput, calls=%fused_computation.39 | convolution fusion | flops 1629749248 | bytes 1372168 | tf_op jit(solution)/shard_map/clnp,lnpq->clq/dot_general | solution.py:90
  303.7 3.3 %scatter_custom_fusion = f32[64,1024]{0,1:T(8,128)S(1)} fusion(s32[1024]{0:T(1024)} %get-tuple-element.108, f32[1024,64]{1,0:T(8,128)S(1)} %copy.49, f32[]{:T(128)} %constant.109.clone.1), kind=kCustom, calls=%fused_computation.71 | custom fusion | bytes 262656 | tf_op jit(solution)/shard_map/scatter | solution.py:164
  (183 shorter events, 97.9 us)
Async XLA Ops:
  6.5 44.5 %copy-start = (f32[4,256,256]{2,1,0:T(8,128)S(1)}, f32[4,256,256]{2,1,0:T(8,128)}, u32[]{:S(2)}) copy-start(f32[4,256,256]{2,1,0:T(8,128)} %param.26) | copy-start | bytes 3145732
  6.5 38.6 %reduce-scatter.3.cloned.1.call-start = ((), (), s32[]{:S(2)}) async-start(), calls=%async_computation.2 | async-start | bytes 98304 | tf_op jit(solution)/shard_map/reduce_scatter | solution.py:66
  13.2 16.3 %copy-start.19 = (s32[1,8]{1,0:T(1,128)S(1)}, s32[1,8]{1,0:T(1,128)}, u32[]{:S(2)}) copy-start(s32[1,8]{1,0:T(1,128)} %param.23) | copy-start | bytes 100
  13.2 16.8 %copy-start.17 = (s32[2,4]{1,0:T(2,128)S(1)}, s32[2,4]{1,0:T(2,128)}, u32[]{:S(2)}) copy-start(s32[2,4]{1,0:T(2,128)} %param.21) | copy-start | bytes 100
  15.3 28.4 %collective-permute-start.5 = (f32[2,64,256]{2,1,0:T(8,128)S(1)}, f32[2,64,256]{2,1,0:T(8,128)S(1)}, u32[]{:S(2)}, u32[]{:S(2)}) collective-permute-start(f32[2,64,256]{2,1,0:T(8,128)S(1)} %fusion.58), channel_id=1, source_target_pairs={{1,0},{2,1},{3,2},{4,3},{5,4},{6,5},{7,6},{8,7},{9,8},{10,9},{11,1... | collective-permute-start | bytes 393224 | tf_op jit(solution)/shard_map/ppermute | solution.py:15
  16.0 27.7 %collective-permute-start.4 = (f32[2,64,256]{2,1,0:T(8,128)S(1)}, f32[2,64,256]{2,1,0:T(8,128)S(1)}, u32[]{:S(2)}, u32[]{:S(2)}) collective-permute-start(f32[2,64,256]{2,1,0:T(8,128)S(1)} %fusion.58), channel_id=1, source_target_pairs={{31,0},{0,1},{1,2},{2,3},{3,4},{4,5},{5,6},{6,7},{7,8},{8,9},{9,10... | collective-permute-start | bytes 393224 | tf_op jit(solution)/shard_map/ppermute | solution.py:15
  22.8 13.8 %collective-permute-start.1 = (f32[3,1024]{0,1:T(8,128)S(1)}, f32[3,1024]{0,1:T(8,128)}, u32[]{:S(2)}, u32[]{:S(2)}) collective-permute-start(f32[3,1024]{0,1:T(8,128)S(1)} %bitcast.164), channel_id=1, source_target_pairs={{1,0},{2,1},{3,2},{4,3},{5,4},{6,5},{7,6},{8,7},{9,8},{10,9},{11,1... | collective-permute-start | bytes 36872 | tf_op jit(solution)/shard_map/ppermute | solution.py:15
  22.8 16.7 %collective-permute-start = (f32[3,1024]{0,1:T(8,128)S(1)}, f32[3,1024]{0,1:T(8,128)}, u32[]{:S(2)}, u32[]{:S(2)}) collective-permute-start(f32[3,1024]{0,1:T(8,128)S(1)} %bitcast.165), channel_id=1, source_target_pairs={{31,0},{0,1},{1,2},{2,3},{3,4},{4,5},{5,6},{6,7},{7,8},{8,9},{9,10... | collective-permute-start | bytes 36872 | tf_op jit(solution)/shard_map/ppermute | solution.py:15
  25.6 182.6 %reduce-scatter.5.cloned.1.call-start = ((), (), s32[]{:S(2)}) async-start(), calls=%async_computation.3 | async-start | bytes 98304 | tf_op jit(solution)/shard_map/reduce_scatter | solution.py:66
  25.7 107.0 %collective-permute-start.3 = (f32[64,1024]{0,1:T(8,128)}, f32[64,1024]{0,1:T(8,128)}, u32[]{:S(2)}, u32[]{:S(2)}) collective-permute-start(f32[64,1024]{0,1:T(8,128)} %bitcast.171), channel_id=1, source_target_pairs={{1,0},{2,1},{3,2},{4,3},{5,4},{6,5},{7,6},{8,7},{9,8},{10,9},{11,1... | collective-permute-start | bytes 786440 | tf_op jit(solution)/shard_map/ppermute | solution.py:15
  36.6 96.1 %collective-permute-start.2 = (f32[64,1024]{0,1:T(8,128)}, f32[64,1024]{0,1:T(8,128)}, u32[]{:S(2)}, u32[]{:S(2)}) collective-permute-start(f32[64,1024]{0,1:T(8,128)} %bitcast.172), channel_id=1, source_target_pairs={{31,0},{0,1},{1,2},{2,3},{3,4},{4,5},{5,6},{6,7},{7,8},{8,9},{9,10... | collective-permute-start | bytes 786440 | tf_op jit(solution)/shard_map/ppermute | solution.py:15
  45.1 9.7 %collective-permute-start.6 = (f32[32,256]{1,0:T(8,128)}, f32[32,256]{1,0:T(8,128)S(1)}, u32[]{:S(2)}, u32[]{:S(2)}) collective-permute-start(f32[32,256]{1,0:T(8,128)} %reduce-scatter.3.cloned.1.call-done), channel_id=1, source_target_pairs={{4,0},{6,2},{8,4},{10,6},{12,8},{14,10},{16,12},{18,14},{20,16},{2... | collective-permute-start | bytes 98312 | tf_op jit(solution)/shard_map/ppermute | solution.py:15
  51.8 80.9 %copy-start.3 = (f32[1024,64]{1,0:T(8,128)S(1)}, f32[1024,64]{1,0:T(8,128)}, u32[]{:S(2)}) copy-start(f32[1024,64]{1,0:T(8,128)} %gather_fusion.2) | copy-start | bytes 786436
  51.8 34.6 %collective-permute-start.13 = (f32[32,256]{1,0:T(8,128)}, f32[32,256]{1,0:T(8,128)S(1)}, u32[]{:S(2)}, u32[]{:S(2)}) collective-permute-start(f32[32,256]{1,0:T(8,128)} %reduce-scatter.3.cloned.1.call-done), channel_id=1, source_target_pairs={{22,0},{24,2},{26,4},{28,6},{30,8},{0,10},{2,12},{4,14},{6,16},{8,... | collective-permute-start | bytes 98312 | tf_op jit(solution)/shard_map/ppermute | solution.py:15
  53.5 32.9 %collective-permute-start.12 = (f32[32,256]{1,0:T(8,128)}, f32[32,256]{1,0:T(8,128)S(1)}, u32[]{:S(2)}, u32[]{:S(2)}) collective-permute-start(f32[32,256]{1,0:T(8,128)} %reduce-scatter.3.cloned.1.call-done), channel_id=1, source_target_pairs={{24,0},{26,2},{28,4},{30,6},{0,8},{2,10},{4,12},{6,14},{8,16},{10,... | collective-permute-start | bytes 98312 | tf_op jit(solution)/shard_map/ppermute | solution.py:15
  54.8 12.3 %collective-permute-start.7 = (f32[32,256]{1,0:T(8,128)}, f32[32,256]{1,0:T(8,128)S(1)}, u32[]{:S(2)}, u32[]{:S(2)}) collective-permute-start(f32[32,256]{1,0:T(8,128)} %reduce-scatter.3.cloned.1.call-done), channel_id=1, source_target_pairs={{6,0},{8,2},{10,4},{12,6},{14,8},{16,10},{18,12},{20,14},{22,16},{... | collective-permute-start | bytes 98312 | tf_op jit(solution)/shard_map/ppermute | solution.py:15
  67.1 3.4 %collective-permute-start.8 = (f32[32,256]{1,0:T(8,128)}, f32[32,256]{1,0:T(8,128)S(1)}, u32[]{:S(2)}, u32[]{:S(2)}) collective-permute-start(f32[32,256]{1,0:T(8,128)} %reduce-scatter.3.cloned.1.call-done), channel_id=1, source_target_pairs={{8,0},{10,2},{12,4},{14,6},{16,8},{18,10},{20,12},{22,14},{24,16},... | collective-permute-start | bytes 98312 | tf_op jit(solution)/shard_map/ppermute | solution.py:15
  70.5 6.4 %collective-permute-start.9 = (f32[32,256]{1,0:T(8,128)}, f32[32,256]{1,0:T(8,128)S(1)}, u32[]{:S(2)}, u32[]{:S(2)}) collective-permute-start(f32[32,256]{1,0:T(8,128)} %reduce-scatter.3.cloned.1.call-done), channel_id=1, source_target_pairs={{10,0},{12,2},{14,4},{16,6},{18,8},{20,10},{22,12},{24,14},{26,16}... | collective-permute-start | bytes 98312 | tf_op jit(solution)/shard_map/ppermute | solution.py:15
  77.0 3.3 %collective-permute-start.10 = (f32[32,256]{1,0:T(8,128)}, f32[32,256]{1,0:T(8,128)S(1)}, u32[]{:S(2)}, u32[]{:S(2)}) collective-permute-start(f32[32,256]{1,0:T(8,128)} %reduce-scatter.3.cloned.1.call-done), channel_id=1, source_target_pairs={{28,0},{30,2},{0,4},{2,6},{4,8},{6,10},{8,12},{10,14},{12,16},{14,... | collective-permute-start | bytes 98312 | tf_op jit(solution)/shard_map/ppermute | solution.py:15
  80.3 6.1 %collective-permute-start.11 = (f32[32,256]{1,0:T(8,128)}, f32[32,256]{1,0:T(8,128)S(1)}, u32[]{:S(2)}, u32[]{:S(2)}) collective-permute-start(f32[32,256]{1,0:T(8,128)} %reduce-scatter.3.cloned.1.call-done), channel_id=1, source_target_pairs={{26,0},{28,2},{30,4},{0,6},{2,8},{4,10},{6,12},{8,14},{10,16},{12,... | collective-permute-start | bytes 98312 | tf_op jit(solution)/shard_map/ppermute | solution.py:15
  181.2 12.5 %collective-permute-start.17 = (f32[2,64,256]{2,1,0:T(8,128)S(1)}, f32[2,64,256]{2,1,0:T(8,128)S(1)}, u32[]{:S(2)}, u32[]{:S(2)}) collective-permute-start(f32[2,64,256]{2,1,0:T(8,128)S(1)} %fusion.41), channel_id=1, source_target_pairs={{1,0},{2,1},{3,2},{4,3},{5,4},{6,5},{7,6},{8,7},{9,8},{10,9},{11,1... | collective-permute-start | bytes 393224 | tf_op jit(solution)/shard_map/ppermute | solution.py:15
  188.4 5.3 %collective-permute-start.16 = (f32[2,64,256]{2,1,0:T(8,128)S(1)}, f32[2,64,256]{2,1,0:T(8,128)}, u32[]{:S(2)}, u32[]{:S(2)}) collective-permute-start(f32[2,64,256]{2,1,0:T(8,128)S(1)} %fusion.41), channel_id=1, source_target_pairs={{31,0},{0,1},{1,2},{2,3},{3,4},{4,5},{5,6},{6,7},{7,8},{8,9},{9,10... | collective-permute-start | bytes 393224 | tf_op jit(solution)/shard_map/ppermute | solution.py:15
  190.9 98.6 %collective-permute-start.15 = (f32[64,1024]{1,0:T(8,128)}, f32[64,1024]{1,0:T(8,128)}, u32[]{:S(2)}, u32[]{:S(2)}) collective-permute-start(f32[64,1024]{1,0:T(8,128)} %broadcast_multiply_fusion), channel_id=1, source_target_pairs={{1,0},{2,1},{3,2},{4,3},{5,4},{6,5},{7,6},{8,7},{9,8},{10,9},{11,1... | collective-permute-start | bytes 786440 | tf_op jit(solution)/shard_map/ppermute | solution.py:15
  190.9 98.6 %collective-permute-start.14 = (f32[64,1024]{1,0:T(8,128)}, f32[64,1024]{1,0:T(8,128)}, u32[]{:S(2)}, u32[]{:S(2)}) collective-permute-start(f32[64,1024]{1,0:T(8,128)} %broadcast_multiply_fusion), channel_id=1, source_target_pairs={{31,0},{0,1},{1,2},{2,3},{3,4},{4,5},{5,6},{6,7},{7,8},{8,9},{9,10... | collective-permute-start | bytes 786440 | tf_op jit(solution)/shard_map/ppermute | solution.py:15
  208.2 4.4 %collective-permute-start.18 = (f32[32,256]{1,0:T(8,128)}, f32[32,256]{1,0:T(8,128)S(1)}, u32[]{:S(2)}, u32[]{:S(2)}) collective-permute-start(f32[32,256]{1,0:T(8,128)} %reduce-scatter.5.cloned.1.call-done), channel_id=1, source_target_pairs={{4,0},{6,2},{8,4},{10,6},{12,8},{14,10},{16,12},{18,14},{20,16},{2... | collective-permute-start | bytes 98312 | tf_op jit(solution)/shard_map/ppermute | solution.py:15
  208.9 29.8 %collective-permute-start.25 = (f32[32,256]{1,0:T(8,128)}, f32[32,256]{1,0:T(8,128)S(1)}, u32[]{:S(2)}, u32[]{:S(2)}) collective-permute-start(f32[32,256]{1,0:T(8,128)} %reduce-scatter.5.cloned.1.call-done), channel_id=1, source_target_pairs={{22,0},{24,2},{26,4},{28,6},{30,8},{0,10},{2,12},{4,14},{6,16},{8,... | collective-permute-start | bytes 98312 | tf_op jit(solution)/shard_map/ppermute | solution.py:15
  211.4 27.4 %collective-permute-start.24 = (f32[32,256]{1,0:T(8,128)}, f32[32,256]{1,0:T(8,128)S(1)}, u32[]{:S(2)}, u32[]{:S(2)}) collective-permute-start(f32[32,256]{1,0:T(8,128)} %reduce-scatter.5.cloned.1.call-done), channel_id=1, source_target_pairs={{24,0},{26,2},{28,4},{30,6},{0,8},{2,10},{4,12},{6,14},{8,16},{10,... | collective-permute-start | bytes 98312 | tf_op jit(solution)/shard_map/ppermute | solution.py:15
  212.6 6.6 %collective-permute-start.19 = (f32[32,256]{1,0:T(8,128)}, f32[32,256]{1,0:T(8,128)S(1)}, u32[]{:S(2)}, u32[]{:S(2)}) collective-permute-start(f32[32,256]{1,0:T(8,128)} %reduce-scatter.5.cloned.1.call-done), channel_id=1, source_target_pairs={{6,0},{8,2},{10,4},{12,6},{14,8},{16,10},{18,12},{20,14},{22,16},{... | collective-permute-start | bytes 98312 | tf_op jit(solution)/shard_map/ppermute | solution.py:15
  219.2 5.8 %collective-permute-start.20 = (f32[32,256]{1,0:T(8,128)}, f32[32,256]{1,0:T(8,128)S(1)}, u32[]{:S(2)}, u32[]{:S(2)}) collective-permute-start(f32[32,256]{1,0:T(8,128)} %reduce-scatter.5.cloned.1.call-done), channel_id=1, source_target_pairs={{8,0},{10,2},{12,4},{14,6},{16,8},{18,10},{20,12},{22,14},{24,16},... | collective-permute-start | bytes 98312 | tf_op jit(solution)/shard_map/ppermute | solution.py:15
  225.0 4.0 %collective-permute-start.21 = (f32[32,256]{1,0:T(8,128)}, f32[32,256]{1,0:T(8,128)S(1)}, u32[]{:S(2)}, u32[]{:S(2)}) collective-permute-start(f32[32,256]{1,0:T(8,128)} %reduce-scatter.5.cloned.1.call-done), channel_id=1, source_target_pairs={{10,0},{12,2},{14,4},{16,6},{18,8},{20,10},{22,12},{24,14},{26,16}... | collective-permute-start | bytes 98312 | tf_op jit(solution)/shard_map/ppermute | solution.py:15
  229.0 3.2 %collective-permute-start.22 = (f32[32,256]{1,0:T(8,128)}, f32[32,256]{1,0:T(8,128)S(1)}, u32[]{:S(2)}, u32[]{:S(2)}) collective-permute-start(f32[32,256]{1,0:T(8,128)} %reduce-scatter.5.cloned.1.call-done), channel_id=1, source_target_pairs={{28,0},{30,2},{0,4},{2,6},{4,8},{6,10},{8,12},{10,14},{12,16},{14,... | collective-permute-start | bytes 98312 | tf_op jit(solution)/shard_map/ppermute | solution.py:15
  232.1 6.6 %collective-permute-start.23 = (f32[32,256]{1,0:T(8,128)}, f32[32,256]{1,0:T(8,128)S(1)}, u32[]{:S(2)}, u32[]{:S(2)}) collective-permute-start(f32[32,256]{1,0:T(8,128)} %reduce-scatter.5.cloned.1.call-done), channel_id=1, source_target_pairs={{26,0},{28,2},{30,4},{0,6},{2,8},{4,10},{6,12},{8,14},{10,16},{12,... | collective-permute-start | bytes 98312 | tf_op jit(solution)/shard_map/ppermute | solution.py:15
  (17 other events, 66.8 us)
Sparse Core Ops, SparseCore 0:
  25.7 16.0 reduce-scatter.2
  193.8 14.3 reduce-scatter.4
